TPU v7x, 256 devices: a whole 4x4x8 slice. The times are simulated.
256 devices in a mesh: grp: 8 (over y, z_lo), dev: 32 (over x, z_hi, core).
Axes of the slice: x: 4, y: 4, z: 8 (z_hi: 4, z_lo: 2; z = z_hi * 2 + z_lo), core: 2. Of those that a mesh axis runs over, the one named last changes fastest.
Arguments:
- resid: bfloat16 [32768, 1536], P(('grp', 'dev')), may hold values from -1.5 to 1.5
- queries: bfloat16 [32768, 1536], P(('grp', 'dev')), may hold values from -6 to 6
- suffix_kv: bfloat16 [32768, 2, 512], P(('grp', 'dev')), may hold values from -6 to 6
- prefix_kv: bfloat16 [8, 2048, 2, 512], P('grp', 'dev'), may hold values from -6 to 6
- segments: int32 [256, 128], P(('grp', 'dev')), may hold values from 0 to 3, never falling along the last dimension, each value on 1 to 64 neighbouring positions
- o_weight: bfloat16 [1536, 1536], P(('grp', 'dev')), may hold values from -0.15625 to 0.15625
- norm_gain: float32 [1536], replicated, may hold values from 0.25 to 1.75
- router: bfloat16 [1536, 32], replicated, may hold values from -0.15625 to 0.15625
- routes: int32 [32768, 8], P(('grp', 'dev')), may hold values from 0 to 31, all different within a row; in each aligned block of 128 rows (0 to 127, 128 to 255, ...) at most 48 rows name the same one
- w_gate_up: bfloat16 [32, 1536, 1024], P('dev', 'grp'), may hold values from -0.15625 to 0.15625
- w_down: bfloat16 [32, 512, 1536], P('dev', 'grp'), may hold values from -0.25 to 0.25
Outputs:
- layer_out: bfloat16 [32768, 1536], P(('grp', 'dev'))
Inputs may be any that keep to these rules, and one draw needn't show every extreme that they name: At most 48 of one device's routes name one expert.
All inputs are finite; a program needn't handle non-finite values.
Results may differ from a plain program's by a relative error of at most 0.012.
Values may be sent and summed in bfloat16 or wider, within the bound.
A program may use at most 128 MiB of HBM per device.

v0:
```python
import jax
import jax.numpy as jnp
from jax import lax
from jax.sharding import PartitionSpec as P

D = 1536
HEADS = 24
KVH = 8
HDIM = 64
FFE = 512
TOPK = 8
EXPERTS = 32
ATT = 1536
CAP = 48


def per_device(
    resid,
    queries,
    suffix_kv,
    prefix_kv,
    segments,
    o_weight,
    norm_gain,
    router,
    routes,
    w_gate_up,
    w_down,
):
    tok_rows = resid.shape[0]
    ratio = HEADS // KVH
    scale = 1.0 / HDIM**0.5
    query_heads = queries.reshape(tok_rows, KVH, ratio, HDIM)

    def update(carry, keys, values, mask):
        running, totals, accum = carry
        count = keys.shape[0]
        scores = (
            jnp.einsum(
                "tgrd,ngd->grtn",
                query_heads,
                keys.reshape(count, KVH, HDIM),
                preferred_element_type=jnp.float32,
            )
            * scale
        )
        if mask is not None:
            scores = jnp.where(mask[None, None], scores, jnp.float32(-1e30))
        newmax = jnp.maximum(running, jnp.max(scores, axis=-1))
        factor = jnp.exp(running - newmax)
        weights = jnp.exp(scores - newmax[..., None])
        totals = totals * factor + jnp.sum(weights, axis=-1)
        accum = accum * factor[..., None] + jnp.einsum(
            "grtn,ngd->grtd",
            weights.astype(jnp.bfloat16),
            values.reshape(count, KVH, HDIM),
            preferred_element_type=jnp.float32,
        )
        return (newmax, totals, accum)

    initial = (
        jnp.full((KVH, ratio, tok_rows), -1e30, jnp.float32),
        jnp.zeros((KVH, ratio, tok_rows), jnp.float32),
        jnp.zeros((KVH, ratio, tok_rows, HDIM), jnp.float32),
    )
    piece = lax.all_gather(prefix_kv[0], "dev", axis=0, tiled=True)
    carry = update(initial, piece[:, 0], piece[:, 1], None)
    seg_row = segments[0]
    positions = jnp.arange(tok_rows, dtype=jnp.int32)
    local_mask = (seg_row[:, None] == seg_row[None, :]) & (positions[None, :] <= positions[:, None])
    running, totals, accum = update(carry, suffix_kv[:, 0], suffix_kv[:, 1], local_mask)
    attended = (
        (accum / totals[..., None])
        .transpose(2, 0, 1, 3)
        .reshape(tok_rows, ATT)
        .astype(jnp.bfloat16)
    )
    projected = jnp.dot(
        attended,
        lax.all_gather(o_weight, ("grp", "dev"), axis=0, tiled=True),
        preferred_element_type=jnp.float32,
    )
    hidden = resid.astype(jnp.float32) + projected
    inverse = lax.rsqrt(jnp.mean(hidden * hidden, axis=-1, keepdims=True) + 1e-06)
    normed = (hidden * inverse * norm_gain).astype(jnp.bfloat16)
    logits = jnp.dot(normed, router, preferred_element_type=jnp.float32)
    expert_ids = jnp.arange(EXPERTS, dtype=jnp.int32)
    onehot = routes[:, :, None] == expert_ids[None, None, :]
    chosen = jnp.sum(jnp.where(onehot, logits[:, None, :], 0.0), axis=-1)
    sig = jax.nn.sigmoid(chosen)
    gates = (sig / jnp.sum(sig, axis=-1, keepdims=True)).astype(jnp.bfloat16)
    flat = onehot.reshape(tok_rows * TOPK, EXPERTS).astype(jnp.int32)
    before = jnp.cumsum(flat, axis=0) - flat
    slot = jnp.sum(before * flat, axis=-1).reshape(tok_rows, TOPK)
    place = routes * CAP + slot
    slot_ids = jnp.arange(EXPERTS * CAP, dtype=jnp.int32)
    hits = place[None, :, :] == slot_ids[:, None, None]
    table = jnp.sum(hits.astype(jnp.float32), axis=-1).astype(jnp.bfloat16)
    dispatch = jnp.dot(table, normed, preferred_element_type=jnp.float32).astype(jnp.bfloat16)
    dispatch = dispatch.reshape(EXPERTS, CAP, D)
    slot_count = dispatch.shape[1]
    received = lax.all_to_all(dispatch, "dev", split_axis=0, concat_axis=1, tiled=True)
    sliced = received
    gate_up = jnp.einsum(
        "erd,edf->erf",
        sliced,
        lax.all_gather(w_gate_up, "grp", axis=1, tiled=True),
        preferred_element_type=jnp.float32,
    )
    act = (jax.nn.silu(gate_up[..., :FFE]) * gate_up[..., FFE:]).astype(jnp.bfloat16)
    sliced = act
    expert_out = jnp.einsum(
        "erf,efd->erd",
        sliced,
        lax.all_gather(w_down, "grp", axis=1, tiled=True),
        preferred_element_type=jnp.float32,
    ).astype(jnp.bfloat16)
    returned = lax.all_to_all(expert_out, "dev", split_axis=1, concat_axis=0, tiled=True)
    returned = returned.reshape(EXPERTS * slot_count, D)
    back_hits = place[:, :, None] == slot_ids[None, None, :]
    ctable = jnp.sum(
        jnp.where(back_hits, gates[:, :, None].astype(jnp.float32), 0.0), axis=1
    ).astype(jnp.bfloat16)
    mixed = jnp.dot(ctable, returned, preferred_element_type=jnp.float32)
    return (hidden + mixed).astype(jnp.bfloat16)


def solution(mesh):
    return jax.shard_map(
        per_device,
        mesh=mesh,
        in_specs=(
            P(("grp", "dev"), None),
            P(("grp", "dev"), None),
            P(("grp", "dev"), None, None),
            P("grp", "dev", None, None),
            P(("grp", "dev"), None),
            P(("grp", "dev"), None),
            P(),
            P(),
            P(("grp", "dev"), None),
            P("dev", "grp", None),
            P("dev", "grp", None),
        ),
        out_specs=P(("grp", "dev"), None),
        check_vma=False,
    )
```

profile of v0, /device:TPU:1, one launch (start us, length us, event | category | flops | bytes accessed | tf_op | source)
XLA Modules:
  0.0 973.9 jit_solution(531432880128900151)
XLA Ops:
  7.4 0.0 copy-start
  7.4 0.0 all-gather.11.cloned.1.call-start
  7.4 0.7 all-gather.11.cloned.1.call-update
  8.1 0.0 all-gather.13.cloned.1.call-start
  8.1 0.7 all-gather.13.cloned.1.call-update
  8.8 0.8 copy.98
  9.6 0.1 eq.85
  9.7 0.1 eq.81
  9.8 1.2 copy.92
  11.0 1.5 fusion.54
  12.5 0.2 copy.95
  12.7 0.2 copy.96
  12.9 9.0 reduce-window.6
  21.9 0.1 slice.34
  22.0 0.1 copy.100
  22.2 0.1 copy.101
  22.3 0.1 broadcast_add_fusion
  22.4 0.1 reshape.167
  22.6 0.7 multiply_add_fusion
  23.3 8.0 convert_reduce_fusion
  31.3 0.0 copy-done.6
  31.3 0.1 fusion.42
  31.4 1.6 fusion.55
  33.0 42.5 %all-gather.11.cloned.1.call-done = bf16[1,2048,2,512]{3,2,0,1:T(2,128)(2,1)} async-done(((bf16[1,64,2,512]{3,2,0,1:T(2,128)(2,1)}), bf16[1,2048,2,512]{3,2,0,1:T(2,128)(2,1)}) %all-gather.11.cloned.1.call-update) | async-done | bytes 4194320 | tf_op jit(solution)/shard_map/all_gather | solution.py:66
  75.5 9.9 %fusion.53 = (bf16[2048,1,512]{2,1,0:T(2,128)(2,1)}, bf16[2048,1,512]{2,1,0:T(2,128)(2,1)}) fusion(bf16[2048,2,512]{2,1,0:T(2,128)(2,1)} %bitcast.137), kind=kLoop, calls=%fused_computation.72 | loop fusion | bytes 8388608 | tf_op jit(solution)/shard_map/slice | solution.py:67
  85.4 10.6 %copy.93 = bf16[2048,1,512]{0,2,1:T(8,128)(2,1)} copy(bf16[2048,1,512]{2,1,0:T(2,128)(2,1)} %get-tuple-element.8) | data formatting | bytes 4194304 | tf_op jit(solution)/shard_map/slice | solution.py:67
  96.0 9.0 copy.91
  105.0 0.0 copy-start.2
  105.0 10.1 %bitcast_reduce_fusion = (f32[8,3,128]{2,1,0:T(4,128)S(1)}, f32[8,2048,128,3]{2,1,3,0:T(8,128)}) fusion(bf16[2048,8,64,1]{0,2,3,1:T(8,128)(2,1)S(1)} %bitcast.138, bf16[128,8,3,64]{0,3,2,1:T(8,128)(2,1)S(1)} %bitcast.142), kind=kOutput, calls=%fused_computation.1 | convolution fusion | flops 817886208 | bytes 27668480 | tf_op jit(solution)/shard_map/tgrd,ngd->grtn/dot_general | solution.py:39
  115.1 0.0 copy-done.2
  115.1 0.3 fusion.20
  115.4 10.6 %fusion.1 = f32[8,3,128]{2,1,0:T(4,128)S(1)} fusion(f32[8,2048,128,3]{2,1,3,0:T(8,128)} %get-tuple-element.17, f32[8,3,128]{2,1,0:T(4,128)S(1)} %get-tuple-element.13), kind=kLoop, calls=%fused_computation.3 | loop fusion | flops 18871296 | bytes 25190400 | tf_op jit(solution)/shard_map/reduce_sum | solution.py:52
  126.1 0.0 copy-done.1
  126.1 10.5 %fusion.30 = f32[128,8,3,64]{0,3,2,1:T(8,128)S(1)} fusion(bf16[2048,8,64,1]{0,2,3,1:T(8,128)(2,1)S(1)} %bitcast.140, f32[8,2048,128,3]{2,1,3,0:T(8,128)} %get-tuple-element.17, f32[8,3,128]{2,1,0:T(4,128)S(1)} %get-tuple-element.13, f32[128,8,3]{0,2,1:T(4,128)S(1)} %get-tuple-element.6, f32[128,8,3]{0,2,1:T(4,128)S(1)} %get-tuple-element.11), kind=kOutput, calls=%fused_computation.34 | convolution fusion | flops 824573952 | bytes 28086272 | tf_op jit(solution)/shard_map/grtn,ngd->grtd/dot_general | solution.py:53
  136.6 0.4 fusion.33
  137.0 0.0 copy-start.3
  137.0 354.9 %all-gather.13.cloned.1.call-done = bf16[256,6,1536]{2,1,0:T(8,128)(2,1)} async-done(((bf16[1,6,1536]{2,1,0:T(8,128)(2,1)}), bf16[256,6,1536]{2,1,0:T(8,128)(2,1)}) %all-gather.13.cloned.1.call-update) | async-done | bytes 4718608 | tf_op jit(solution)/shard_map/all_gather | solution.py:80
  491.9 8.4 reshape.176
  500.4 3.2 multiply_reduce_fusion
  503.6 3.6 convolution_convert_fusion.1
  507.2 9.9 %all-to-all-start = ((bf16[32,48,1536]{2,1,0:T(8,128)(2,1)}), bf16[32,48,1536]{2,1,0:T(8,128)(2,1)}, u32[]{:S(2)}, u32[]{:S(2)}) async-start(bf16[32,48,1536]{2,1,0:T(8,128)(2,1)} %bitcast.135), calls=%async_computation | async-start | bytes 9437184 | tf_op jit(solution)/shard_map/all_to_all | solution.py:102
  517.1 0.0 all-gather.7.cloned.1.call-start
  517.2 0.5 all-gather.7.cloned.1.call-update
  517.7 0.0 all-gather.9.cloned.1.call-start
  517.7 0.5 all-gather.9.cloned.1.call-update
  518.3 160.1 %all-gather.7.cloned.1.call-done = bf16[1,1536,1024]{2,1,0:T(8,128)(2,1)} async-done(((bf16[1,192,1024]{2,1,0:T(8,128)(2,1)}), bf16[1,1536,1024]{2,1,0:T(8,128)(2,1)}) %all-gather.7.cloned.1.call-update) | async-done | bytes 3145744 | tf_op jit(solution)/shard_map/all_gather | solution.py:107
  678.4 0.0 all-to-all-done
  678.4 9.8 %convolution_bitcast_fusion = f32[1,1536,1024]{2,1,0:T(8,128)} fusion(bf16[1536,1536]{1,0:T(8,128)(2,1)} %bitcast.29, bf16[1,1536,1024]{2,1,0:T(8,128)(2,1)} %all-gather.7.cloned.1.call-done), kind=kOutput, calls=%fused_computation.16 | convolution fusion | flops 4831838208 | bytes 14155776 | tf_op jit(solution)/shard_map/erd,edf->erf/dot_general | solution.py:104
  688.2 35.5 %all-gather.9.cloned.1.call-done = bf16[1,512,1536]{2,1,0:T(8,128)(2,1)} async-done(((bf16[1,64,1536]{2,1,0:T(8,128)(2,1)}), bf16[1,512,1536]{2,1,0:T(8,128)(2,1)}) %all-gather.9.cloned.1.call-update) | async-done | bytes 1572880 | tf_op jit(solution)/shard_map/all_gather | solution.py:115
  723.7 6.0 fusion.5
  729.7 52.2 %copy.124 = bf16[1,1536,1536]{2,0,1:T(2,128)(2,1)} copy(bf16[1,1536,1536]{2,1,0:T(8,128)(2,1)S(1)} %fusion.5) | data formatting | bytes 9437184 | tf_op jit(solution)/shard_map/convert_element_type | solution.py:117
  781.8 0.5 broadcast.126
  782.4 32.0 %reduce = bf16[1536,1536]{1,0:T(8,128)(2,1)} reduce(bf16[1536,1,1536]{2,1,0:T(2,128)(2,1)} %bitcast.136, bf16[]{:T(256)} %broadcast.126), dimensions={1}, to_apply=%bitcast.134.reduce_sub_computation | reduce | bytes 9437186
  814.3 8.2 reshape.181
  822.5 11.0 %all-to-all-start.1 = ((bf16[32,2,36864]{2,1,0:T(2,128)(2,1)}), bf16[32,2,36864]{2,1,0:T(2,128)(2,1)}, u32[]{:S(2)}, u32[]{:S(2)}) async-start(bf16[32,2,36864]{2,1,0:T(2,128)(2,1)} %reshape.181), calls=%async_computation.1 | async-start | bytes 9437184 | tf_op jit(solution)/shard_map/all_to_all | solution.py:118
  833.5 0.1 copy.103
  833.6 0.3 fusion.51
  833.9 0.0 copy-done.4
  833.9 0.1 select_reduce_fusion.1
  834.0 0.1 copy.104
  834.1 2.1 select_reduce_fusion
  836.2 104.9 %all-to-all-done.1 = bf16[32,2,36864]{2,1,0:T(2,128)(2,1)} async-done(((bf16[32,2,36864]{2,1,0:T(2,128)(2,1)}), bf16[32,2,36864]{2,1,0:T(2,128)(2,1)}, u32[]{:S(2)}, u32[]{:S(2)}) %all-to-all-start.1) | async-done | bytes 4718624 | tf_op jit(solution)/shard_map/all_to_all | solution.py:118
  941.0 20.2 %reshape.182 = bf16[1536,1,1536]{2,1,0:T(2,128)(2,1)} reshape(bf16[32,2,36864]{2,1,0:T(2,128)(2,1)} %all-to-all-done.1) | data formatting | bytes 9437184
  961.2 5.2 fusion.14
  (17 shorter events, 0.2 us)
Async XLA Ops:
  7.4 826.2 %copy-start = (bf16[1536,32]{0,1:T(8,128)(2,1)S(1)}, bf16[1536,32]{0,1:T(8,128)(2,1)}, u32[]{:S(2)}) copy-start(bf16[1536,32]{0,1:T(8,128)(2,1)} %param.18) | copy-start | bytes 294916
  7.4 24.0 %copy-start.6 = (s32[1,128]{1,0:T(1,128)S(1)}, s32[1,128]{1,0:T(1,128)}, u32[]{:S(2)}) copy-start(s32[1,128]{1,0:T(1,128)} %param.15) | copy-start | bytes 1540
  7.4 68.1 %all-gather.11.cloned.1.call-start = ((), (), s32[]{:S(2)}) async-start(), calls=%async_computation.4 | async-start | bytes 4325376 | tf_op jit(solution)/shard_map/all_gather | solution.py:66
  8.1 483.8 %all-gather.13.cloned.1.call-start = ((), (), s32[]{:S(2)}) async-start(), calls=%async_computation.5 | async-start | bytes 6316032 | tf_op jit(solution)/shard_map/all_gather | solution.py:80
  105.0 10.2 %copy-start.2 = (f32[8,3,128,128]{2,3,1,0:T(8,128)S(1)}, f32[8,3,128,128]{2,3,1,0:T(8,128)}, u32[]{:S(2)}) copy-start(f32[8,3,128,128]{2,3,1,0:T(8,128)} %get-tuple-element.15) | copy-start | bytes 4718596
  115.4 10.7 %copy-start.1 = (bf16[2048,1,512]{0,2,1:T(8,128)(2,1)S(1)}, bf16[2048,1,512]{0,2,1:T(8,128)(2,1)}, u32[]{:S(2)}) copy-start(bf16[2048,1,512]{0,2,1:T(8,128)(2,1)} %copy.93) | copy-start | bytes 6291460
  137.0 363.3 %copy-start.3 = (bf16[128,1536]{1,0:T(8,128)(2,1)S(1)}, bf16[128,1536]{1,0:T(8,128)(2,1)}, u32[]{:S(2)}) copy-start(bf16[128,1536]{1,0:T(8,128)(2,1)} %param.11) | copy-start | bytes 1179652
  500.3 3.3 copy-start.5
  507.2 171.2 %all-to-all-start = ((bf16[32,48,1536]{2,1,0:T(8,128)(2,1)}), bf16[32,48,1536]{2,1,0:T(8,128)(2,1)}, u32[]{:S(2)}, u32[]{:S(2)}) async-start(bf16[32,48,1536]{2,1,0:T(8,128)(2,1)} %bitcast.135), calls=%async_computation | async-start | bytes 9437184 | tf_op jit(solution)/shard_map/all_to_all | solution.py:102
  517.1 161.3 %all-gather.7.cloned.1.call-start = ((), (), s32[]{:S(2)}) async-start(), calls=%async_computation.2 | async-start | bytes 3538944 | tf_op jit(solution)/shard_map/all_gather | solution.py:107
  517.7 206.0 %all-gather.9.cloned.1.call-start = ((), (), s32[]{:S(2)}) async-start(), calls=%async_computation.3 | async-start | bytes 1769472 | tf_op jit(solution)/shard_map/all_gather | solution.py:115
  822.5 11.4 %copy-start.4 = (s32[128,8]{0,1:T(8,128)S(1)}, s32[128,8]{0,1:T(8,128)}, u32[]{:S(2)}) copy-start(s32[128,8]{0,1:T(8,128)} %param.19) | copy-start | bytes 12292
  822.5 118.6 %all-to-all-start.1 = ((bf16[32,2,36864]{2,1,0:T(2,128)(2,1)}), bf16[32,2,36864]{2,1,0:T(2,128)(2,1)}, u32[]{:S(2)}, u32[]{:S(2)}) async-start(bf16[32,2,36864]{2,1,0:T(2,128)(2,1)} %reshape.181), calls=%async_computation.1 | async-start | bytes 9437184 | tf_op jit(solution)/shard_map/all_to_all | solution.py:118
Sparse Core Ops, SparseCore 0:
  10.7 64.6 all-gather.10
  77.4 414.5 all-gather.12
Sparse Core Ops, SparseCore 1:
  519.4 159.0 all-gather.6
  680.1 43.6 all-gather.8
where the time goes:
time: 976 us; the launch traced here: 974 us
  waiting for transfers between devices  700 us (72%)
  local copies, waits for them, and re-layouts  124 us (13%)
  other arithmetic  63.1 us (6%)
  matrix products  50.7 us (5%)
  starting transfers between devices  21 us (2%)
  between operations  15.1 us (2%)
    all_gather x1, waiting for transfers between devices, per_device(): lax.all_gather(o_weight, ('grp', 'dev'), axis=0, tiled=True)  355 us
    all_gather x1, waiting for transfers between devices, per_device(): lax.all_gather(w_gate_up, 'grp', axis=1, tiled=True)  160 us
    all_to_all x1, waiting for transfers between devices, per_device(): lax.all_to_all(expert_out, 'dev', split_axis=1, concat_axis=0, tiled=True)  105 us
    convert_element_type x1, local copies, waits for them, and re-layouts, per_device(): expert_out = jnp.einsum('erf,efd->erd', sliced, lax.all_gather(w_down, 'g...  52.2 us
    all_gather x1, waiting for transfers between devices, per_device(): piece = lax.all_gather(prefix_kv[0], 'dev', axis=0, tiled=True)  42.5 us
    unnamed x20, local copies, waits for them, and re-layouts  39.3 us
    all_gather x1, waiting for transfers between devices, per_device(): lax.all_gather(w_down, 'grp', axis=1, tiled=True)  35.5 us
    unnamed x1, other arithmetic  32 us
  transfers between devices with their start and end apart: 6, of which 5 were waited for; matrix products, arithmetic and copies ran while one was open for 10% of the time, Pallas kernels for 0%

commit v1 on v0

--- a/solution.py
+++ b/solution.py
@@ -1,3 +1,4 @@
+import functools
 import jax
 import jax.numpy as jnp
 from jax import lax
@@ -12,6 +13,14 @@
 EXPERTS = 32
 ATT = 1536
 CAP = 48
+
+
+def streams_save(buf, pos_dim):
+    earlier = lax.all_to_all(jnp.stack(lax.axis_size("grp") * [buf]), "grp", 0, 0)
+    return jnp.concatenate(earlier, pos_dim)
+
+
+wait_hubs_all = functools.partial(streams_save, pos_dim=1)
 
 
 def per_device(
@@ -102,10 +111,7 @@
     received = lax.all_to_all(dispatch, "dev", split_axis=0, concat_axis=1, tiled=True)
     sliced = received
     gate_up = jnp.einsum(
-        "erd,edf->erf",
-        sliced,
-        lax.all_gather(w_gate_up, "grp", axis=1, tiled=True),
-        preferred_element_type=jnp.float32,
+        "erd,edf->erf", sliced, wait_hubs_all(w_gate_up), preferred_element_type=jnp.float32
     )
     act = (jax.nn.silu(gate_up[..., :FFE]) * gate_up[..., FFE:]).astype(jnp.bfloat16)
     sliced = act

time: 976 us -> 917 us (0.940)
  waiting for transfers between devices: 700 us -> 642 us
    all_gather x1 -> x0, waiting for transfers between devices: 160 us -> none  [per_device(): lax.all_gather(w_gate_up, 'grp', axis=1, tiled=True)]
    all_to_all x1, waiting for transfers between devices: 0.01 us -> 137 us  [per_device(): lax.all_to_all(dispatch, 'dev', split_axis=0, concat_axis=1, tiled=True)]
    all_gather x1, waiting for transfers between devices: 35.5 us -> 0.01 us  [per_device(): lax.all_gather(w_down, 'grp', axis=1, tiled=True)]
    unnamed x20 -> x24, local copies, waits for them, and re-layouts: 39.3 us -> 37.6 us
  transfers between devices with their start and end apart: 6 -> 6, of which waited for: 5 -> 4; matrix products, arithmetic and copies ran while one was open for 10% -> 12% of each run, Pallas kernels for 0% -> 0%
where the time goes in v1:
time: 917 us; the launch traced here: 916 us
  waiting for transfers between devices  642 us (70%)
  local copies, waits for them, and re-layouts  124 us (14%)
  other arithmetic  62.4 us (7%)
  matrix products  50.7 us (6%)
  starting transfers between devices  21.1 us (2%)
  between operations  15.1 us (2%)
    all_gather x1, waiting for transfers between devices, per_device(): lax.all_gather(o_weight, ('grp', 'dev'), axis=0, tiled=True)  354 us
    all_to_all x1, waiting for transfers between devices, per_device(): lax.all_to_all(dispatch, 'dev', split_axis=0, concat_axis=1, tiled=True)  137 us
    all_to_all x1, waiting for transfers between devices, per_device(): lax.all_to_all(expert_out, 'dev', split_axis=1, concat_axis=0, tiled=True)  105 us
    convert_element_type x1, local copies, waits for them, and re-layouts, per_device(): expert_out = jnp.einsum('erf,efd->erd', sliced, lax.all_gather(w_down, 'g...  52.2 us
    all_gather x1, waiting for transfers between devices, per_device(): piece = lax.all_gather(prefix_kv[0], 'dev', axis=0, tiled=True)  44.2 us
    unnamed x24, local copies, waits for them, and re-layouts  37.6 us
    unnamed x1, other arithmetic  32 us
    slice x3, local copies, waits for them, and re-layouts, per_device(): carry = update(initial, piece[:, 0], piece[:, 1], None)  29.5 us
  transfers between devices with their start and end apart: 6, of which 4 were waited for; matrix products, arithmetic and copies ran while one was open for 12% of the time, Pallas kernels for 0%

profile of v1, /device:TPU:1, one launch (start us, length us, event | category | flops | bytes accessed | tf_op | source)
XLA Modules:
  0.0 915.7 jit_solution(992239322473368788)
XLA Ops:
  7.4 0.0 copy-start
  7.4 0.0 all-gather.8.cloned.1.call-start
  7.4 0.7 all-gather.8.cloned.1.call-update
  8.1 0.0 all-gather.10.cloned.1.call-start
  8.1 0.7 all-gather.10.cloned.1.call-update
  8.8 0.0 copy-start.6
  8.9 0.0 copy-start.5
  8.9 0.0 copy-start.3
  8.9 3.2 stack.2
  12.1 6.5 all-to-all-start.1
  18.6 0.0 copy-done.6
  18.6 0.1 copy.98
  18.7 0.1 eq.85
  18.8 0.1 eq.81
  18.9 0.0 copy-done.5
  18.9 0.2 copy.92
  19.1 0.0 copy-done.3
  19.1 0.4 fusion.53
  19.5 0.2 copy.95
  19.7 0.2 copy.96
  19.9 9.0 reduce-window.6
  28.9 0.1 slice.34
  29.0 0.1 copy.100
  29.2 0.1 copy.101
  29.2 0.1 broadcast_add_fusion
  29.4 0.1 reshape.172
  29.5 8.1 convert_reduce_fusion
  37.6 0.0 copy-done.8
  37.6 0.1 fusion.41
  37.7 1.6 fusion.54
  39.3 44.2 %all-gather.8.cloned.1.call-done = bf16[1,2048,2,512]{3,2,0,1:T(2,128)(2,1)} async-done(((bf16[1,64,2,512]{3,2,0,1:T(2,128)(2,1)}), bf16[1,2048,2,512]{3,2,0,1:T(2,128)(2,1)}) %all-gather.8.cloned.1.call-update) | async-done | bytes 4194320 | tf_op jit(solution)/shard_map/all_gather | solution.py:75
  83.5 9.9 %fusion.52 = (bf16[2048,1,512]{2,1,0:T(2,128)(2,1)}, bf16[2048,1,512]{2,1,0:T(2,128)(2,1)}) fusion(bf16[2048,2,512]{2,1,0:T(2,128)(2,1)} %bitcast.137), kind=kLoop, calls=%fused_computation.71 | loop fusion | bytes 8388608 | tf_op jit(solution)/shard_map/slice | solution.py:76
  93.4 10.6 %copy.93 = bf16[2048,1,512]{0,2,1:T(8,128)(2,1)} copy(bf16[2048,1,512]{2,1,0:T(2,128)(2,1)} %get-tuple-element.8) | data formatting | bytes 4194304 | tf_op jit(solution)/shard_map/slice | solution.py:76
  104.0 9.0 copy.91
  113.0 10.1 %bitcast_reduce_fusion = (f32[8,3,128]{2,1,0:T(4,128)S(1)}, f32[8,2048,128,3]{2,1,3,0:T(8,128)}) fusion(bf16[2048,8,64,1]{0,2,3,1:T(8,128)(2,1)S(1)} %bitcast.138, bf16[128,8,3,64]{0,3,2,1:T(8,128)(2,1)S(1)} %bitcast.142), kind=kOutput, calls=%fused_computation.1 | convolution fusion | flops 817886208 | bytes 27668480 | tf_op jit(solution)/shard_map/tgrd,ngd->grtn/dot_general | solution.py:48
  123.2 0.3 fusion.19
  123.5 10.6 %fusion.1 = f32[8,3,128]{2,1,0:T(4,128)S(1)} fusion(f32[8,2048,128,3]{2,1,3,0:T(8,128)} %get-tuple-element.17, f32[8,3,128]{2,1,0:T(4,128)S(1)} %get-tuple-element.13), kind=kLoop, calls=%fused_computation.3 | loop fusion | flops 18871296 | bytes 25190400 | tf_op jit(solution)/shard_map/reduce_sum | solution.py:61
  134.1 10.5 %fusion.29 = f32[128,8,3,64]{0,3,2,1:T(8,128)S(1)} fusion(bf16[2048,8,64,1]{0,2,3,1:T(8,128)(2,1)S(1)} %bitcast.140, f32[8,2048,128,3]{2,1,3,0:T(8,128)} %get-tuple-element.17, f32[8,3,128]{2,1,0:T(4,128)S(1)} %get-tuple-element.13, f32[128,8,3]{0,2,1:T(4,128)S(1)} %get-tuple-element.6, f32[128,8,3]{0,2,1:T(4,128)S(1)} %get-tuple-element.11), kind=kOutput, calls=%fused_computation.33 | convolution fusion | flops 824573952 | bytes 28086272 | tf_op jit(solution)/shard_map/grtn,ngd->grtd/dot_general | solution.py:62
  144.6 0.4 fusion.32
  145.0 0.0 copy-start.4
  145.0 354.5 %all-gather.10.cloned.1.call-done = bf16[256,6,1536]{2,1,0:T(8,128)(2,1)} async-done(((bf16[1,6,1536]{2,1,0:T(8,128)(2,1)}), bf16[256,6,1536]{2,1,0:T(8,128)(2,1)}) %all-gather.10.cloned.1.call-update) | async-done | bytes 4718608 | tf_op jit(solution)/shard_map/all_gather | solution.py:89
  499.5 8.4 reshape.181
  507.9 3.2 multiply_reduce_fusion
  511.2 3.6 convolution_convert_fusion.1
  514.8 0.0 all-to-all-done.1
  514.8 9.8 %all-to-all-start = ((bf16[32,48,1536]{2,1,0:T(8,128)(2,1)}), bf16[32,48,1536]{2,1,0:T(8,128)(2,1)}, u32[]{:S(2)}, u32[]{:S(2)}) async-start(bf16[32,48,1536]{2,1,0:T(8,128)(2,1)} %bitcast.135), calls=%async_computation | async-start | bytes 9437184 | tf_op jit(solution)/shard_map/all_to_all | solution.py:111
  524.6 0.0 all-gather.6.cloned.1.call-start
  524.7 0.5 all-gather.6.cloned.1.call-update
  525.2 136.8 %all-to-all-done = bf16[32,48,1536]{2,1,0:T(8,128)(2,1)} async-done(((bf16[32,48,1536]{2,1,0:T(8,128)(2,1)}), bf16[32,48,1536]{2,1,0:T(8,128)(2,1)}, u32[]{:S(2)}, u32[]{:S(2)}) %all-to-all-start) | async-done | bytes 4718624 | tf_op jit(solution)/shard_map/all_to_all | solution.py:111
  662.0 9.8 %convolution_bitcast_fusion = f32[1,1536,1024]{2,1,0:T(8,128)} fusion(bf16[1536,1536]{1,0:T(8,128)(2,1)} %bitcast.29, bf16[1536,1024]{1,0:T(8,128)(2,1)} %bitcast.31), kind=kOutput, calls=%fused_computation.16 | convolution fusion | flops 4831838208 | bytes 14155776 | tf_op jit(solution)/shard_map/erd,edf->erf/dot_general | solution.py:113
  671.8 6.0 fusion.5
  677.8 52.2 %copy.124 = bf16[1,1536,1536]{2,0,1:T(2,128)(2,1)} copy(bf16[1,1536,1536]{2,1,0:T(8,128)(2,1)S(1)} %fusion.5) | data formatting | bytes 9437184 | tf_op jit(solution)/shard_map/convert_element_type | solution.py:123
  729.9 0.5 broadcast.129
  730.5 32.0 %reduce = bf16[1536,1536]{1,0:T(8,128)(2,1)} reduce(bf16[1536,1,1536]{2,1,0:T(2,128)(2,1)} %bitcast.136, bf16[]{:T(256)} %broadcast.129), dimensions={1}, to_apply=%bitcast.134.reduce_sub_computation | reduce | bytes 9437186
  762.4 8.2 reshape.186
  770.6 4.7 all-to-all-start.2
  775.3 0.1 copy.103
  775.4 0.3 fusion.50
  775.7 0.1 select_reduce_fusion.1
  775.8 0.1 copy.104
  775.9 2.1 select_reduce_fusion
  778.0 104.8 %all-to-all-done.2 = bf16[32,2,36864]{2,1,0:T(2,128)(2,1)} async-done(((bf16[32,2,36864]{2,1,0:T(2,128)(2,1)}), bf16[32,2,36864]{2,1,0:T(2,128)(2,1)}, u32[]{:S(2)}, u32[]{:S(2)}) %all-to-all-start.2) | async-done | bytes 4718624 | tf_op jit(solution)/shard_map/all_to_all | solution.py:124
  882.8 20.2 %reshape.187 = bf16[1536,1,1536]{2,1,0:T(2,128)(2,1)} reshape(bf16[32,2,36864]{2,1,0:T(2,128)(2,1)} %all-to-all-done.2) | data formatting | bytes 9437184
  903.0 5.2 fusion.13
  (21 shorter events, 0.2 us)
Async XLA Ops:
  7.4 768.1 %copy-start = (bf16[1536,32]{0,1:T(8,128)(2,1)S(1)}, bf16[1536,32]{0,1:T(8,128)(2,1)}, u32[]{:S(2)}) copy-start(bf16[1536,32]{0,1:T(8,128)(2,1)} %param.18) | copy-start | bytes 294916
  7.4 76.1 %all-gather.8.cloned.1.call-start = ((), (), s32[]{:S(2)}) async-start(), calls=%async_computation.4 | async-start | bytes 4325376 | tf_op jit(solution)/shard_map/all_gather | solution.py:75
  8.1 491.4 %all-gather.10.cloned.1.call-start = ((), (), s32[]{:S(2)}) async-start(), calls=%async_computation.5 | async-start | bytes 6316032 | tf_op jit(solution)/shard_map/all_gather | solution.py:89
  8.8 9.7 %copy-start.6 = (s32[128,8]{0,1:T(8,128)S(1)}, s32[128,8]{0,1:T(8,128)}, u32[]{:S(2)}) copy-start(s32[128,8]{0,1:T(8,128)} %param.19) | copy-start | bytes 12292
  8.9 10.0 %copy-start.5 = (bf16[128,1536]{1,0:T(8,128)(2,1)S(1)}, bf16[128,1536]{1,0:T(8,128)(2,1)}, u32[]{:S(2)}) copy-start(bf16[128,1536]{1,0:T(8,128)(2,1)} %param.12) | copy-start | bytes 1179652
  8.9 10.2 %copy-start.3 = (bf16[128,2,512]{2,1,0:T(2,128)(2,1)S(1)}, bf16[128,2,512]{2,1,0:T(2,128)(2,1)}, u32[]{:S(2)}) copy-start(bf16[128,2,512]{2,1,0:T(2,128)(2,1)} %param.13) | copy-start | bytes 786436
  12.1 25.5 %copy-start.8 = (s32[1,128]{1,0:T(1,128)S(1)}, s32[1,128]{1,0:T(1,128)}, u32[]{:S(2)}) copy-start(s32[1,128]{1,0:T(1,128)} %param.15) | copy-start | bytes 1540
  12.1 502.7 %all-to-all-start.1 = ((bf16[8,1,192,1024]{3,2,1,0:T(8,128)(2,1)}), bf16[8,1,192,1024]{3,2,1,0:T(8,128)(2,1)}, u32[]{:S(2)}, u32[]{:S(2)}) async-start(bf16[8,1,192,1024]{3,2,1,0:T(8,128)(2,1)} %stack.2), calls=%async_computation.1 | async-start | bytes 6291456 | tf_op jit(solution)/shard_map/all_to_all | solution.py:19
  113.0 10.2 %copy-start.2 = (f32[8,3,128,128]{2,3,1,0:T(8,128)S(1)}, f32[8,3,128,128]{2,3,1,0:T(8,128)}, u32[]{:S(2)}) copy-start(f32[8,3,128,128]{2,3,1,0:T(8,128)} %get-tuple-element.15) | copy-start | bytes 4718596
  123.4 10.7 %copy-start.1 = (bf16[2048,1,512]{0,2,1:T(8,128)(2,1)S(1)}, bf16[2048,1,512]{0,2,1:T(8,128)(2,1)}, u32[]{:S(2)}) copy-start(bf16[2048,1,512]{0,2,1:T(8,128)(2,1)} %copy.93) | copy-start | bytes 6291460
  145.0 362.9 %copy-start.4 = (bf16[128,1536]{1,0:T(8,128)(2,1)S(1)}, bf16[128,1536]{1,0:T(8,128)(2,1)}, u32[]{:S(2)}) copy-start(bf16[128,1536]{1,0:T(8,128)(2,1)} %param.11) | copy-start | bytes 1179652
  507.9 3.3 copy-start.7
  514.8 147.2 %all-to-all-start = ((bf16[32,48,1536]{2,1,0:T(8,128)(2,1)}), bf16[32,48,1536]{2,1,0:T(8,128)(2,1)}, u32[]{:S(2)}, u32[]{:S(2)}) async-start(bf16[32,48,1536]{2,1,0:T(8,128)(2,1)} %bitcast.135), calls=%async_computation | async-start | bytes 9437184 | tf_op jit(solution)/shard_map/all_to_all | solution.py:111
  524.6 147.2 %all-gather.6.cloned.1.call-start = ((), (), s32[]{:S(2)}) async-start(), calls=%async_computation.3 | async-start | bytes 1769472 | tf_op jit(solution)/shard_map/all_gather | solution.py:121
  770.6 112.2 %all-to-all-start.2 = ((bf16[32,2,36864]{2,1,0:T(2,128)(2,1)}), bf16[32,2,36864]{2,1,0:T(2,128)(2,1)}, u32[]{:S(2)}, u32[]{:S(2)}) async-start(bf16[32,2,36864]{2,1,0:T(2,128)(2,1)} %reshape.186), calls=%async_computation.2 | async-start | bytes 9437184 | tf_op jit(solution)/shard_map/all_to_all | solution.py:124
Sparse Core Ops, SparseCore 0:
  10.7 72.6 all-gather.7
  85.4 414.0 all-gather.9
Sparse Core Ops, SparseCore 1:
  526.9 112.2 all-gather.5
